TPU v7x, 256 devices: a whole 4x4x8 slice. The times are simulated.
256 devices in a mesh: tower: 4 (over x_lo, core), seq: 64 (over x_hi, z, y).
Axes of the slice: x: 4 (x_hi: 2, x_lo: 2; x = x_hi * 2 + x_lo), y: 4, z: 8, core: 2. Of those that a mesh axis runs over, the one named last changes fastest.
Arguments:
- queries: bfloat16 [4, 8192, 3072], P('tower', 'seq'), may hold values from -100 to 100
- keys: bfloat16 [4, 8192, 3072], P('tower', 'seq'), may hold values from -4 to 4
- values: bfloat16 [4, 8192, 3072], P('tower', 'seq'), may hold values from -6 to 6
- alignment: int32 [64, 2], replicated, may hold values from 0 to 192, as said below
- cross_gate: float32 [2, 24], replicated, may hold values from 0.5 to 2
Outputs:
- cross_out: bfloat16 [4, 8192, 3072], P('tower', 'seq')
Inputs may be any that keep to these rules, and one draw needn't show every extreme that they name: `alignment`: lo[a] is max(3a - 1, 0) or max(3a, 0); hi[a] is min(3a + 3, 192) or min(3a + 4, 192).
All inputs are finite; a program needn't handle non-finite values.
Results may differ from a plain program's by a relative error of at most 0.0044.
Values may be sent and summed in bfloat16 or wider, within the bound.
A program may use at most 128 MiB of HBM per device.

v0:
```python
import jax
import jax.numpy as jnp
from jax import lax
from jax.sharding import PartitionSpec as P

HEADS = 24
HEAD_DIM = 128
BLOCK = 128


def from_behind(block, axis, distance):
    devices = range(lax.axis_size(axis))
    route = [(i - distance, i) for i in devices if i - distance in devices]
    return lax.ppermute(block, axis, route)


def attend(query_block, key_rows, value_rows, valid, gain):
    count_q = query_block.shape[0]
    count_k = key_rows.shape[0]
    q_heads = query_block.reshape(count_q, HEADS, HEAD_DIM)
    k_heads = key_rows.reshape(count_k, HEADS, HEAD_DIM)
    v_heads = value_rows.reshape(count_k, HEADS, HEAD_DIM)
    scores = jnp.einsum(
        "qhd,khd->hqk", q_heads, k_heads, preferred_element_type=jnp.float32
    ) * HEAD_DIM ** (-0.5)
    scores = jnp.where(valid[None, None, :], scores, -jnp.inf)
    top = jnp.max(scores, axis=2, keepdims=True)
    weights = jnp.exp(scores - top)
    total = jnp.sum(weights, axis=2)
    rounded = weights.astype(jnp.bfloat16)
    mixed = jnp.einsum("hqk,khd->qhd", rounded, v_heads, preferred_element_type=jnp.float32)
    mixed = mixed / jnp.transpose(total)[:, :, None] * gain[None, :, None]
    return mixed.reshape(count_q, HEADS * HEAD_DIM)


def local(queries, keys, values, alignment, cross_gate):
    rows = queries.shape[1]
    per_dev = rows // BLOCK
    seq_count = lax.axis_size("seq")
    column = lax.axis_index("seq")
    section = lax.axis_index("tower")
    lows = alignment[:, 0]
    highs = alignment[:, 1]
    video_total = 3 * per_dev * seq_count
    audio_total = per_dev * seq_count
    local_queries = queries[0]

    def video_path(audio_keys, audio_values):

        def video_step(block):
            index = per_dev * (3 * column + section) + block
            first = index // 3 - 1
            near = first + jnp.arange(3, dtype=jnp.int32)
            safe = jnp.clip(near, 0, audio_total - 1)
            linked = (
                (near >= 0)
                & (near < audio_total)
                & (jnp.take(lows, safe) <= index)
                & (index < jnp.take(highs, safe))
            )
            return attend(
                local_queries, audio_keys, audio_values, jnp.repeat(linked, BLOCK), cross_gate[0]
            )

        return lax.map(video_step, jnp.arange(per_dev, dtype=jnp.int32))

    key_all, value_all = (
        lax.all_gather(keys, "tower", axis=0, tiled=True),
        lax.all_gather(values, "tower", axis=0, tiled=True),
    )
    lower_pack = jnp.stack(
        [
            jnp.stack([key_all[2, rows - BLOCK :], key_all[3, rows - BLOCK :]]),
            jnp.stack([value_all[2, rows - BLOCK :], value_all[3, rows - BLOCK :]]),
        ]
    )
    upper_pack = jnp.stack(
        [
            jnp.stack([key_all[0, :BLOCK], key_all[3, :BLOCK]]),
            jnp.stack([value_all[0, :BLOCK], value_all[3, :BLOCK]]),
        ]
    )
    lower = from_behind(lower_pack, "seq", 1)
    upper = from_behind(upper_pack, "seq", -1)
    lower_video, lower_audio = (lower[:, 0], lower[:, 1])
    upper_video, upper_audio = (upper[:, 0], upper[:, 1])
    video_keys = jnp.concatenate(
        [lower_video[0], key_all[0], key_all[1], key_all[2], upper_video[0]], axis=0
    )
    video_values = jnp.concatenate(
        [lower_video[1], value_all[0], value_all[1], value_all[2], upper_video[1]], axis=0
    )
    audio_keys = jnp.concatenate([lower_audio[0], key_all[3], upper_audio[0]], axis=0)
    audio_values = jnp.concatenate([lower_audio[1], value_all[3], upper_audio[1]], axis=0)

    def audio_path(unused):

        def audio_step(block):
            index = per_dev * column + block
            first = 3 * index - 1
            near = first + jnp.arange(5, dtype=jnp.int32)
            linked = (
                (near >= 0)
                & (near < video_total)
                & (jnp.take(lows, index) <= near)
                & (near < jnp.take(highs, index))
            )
            return attend(
                local_queries, video_keys, video_values, jnp.repeat(linked, BLOCK), cross_gate[1]
            )

        return lax.map(audio_step, jnp.arange(per_dev, dtype=jnp.int32))

    mixed = lax.cond(
        section == 3, audio_path, lambda unused: video_path(audio_keys, audio_values), 0
    )
    return mixed.astype(jnp.bfloat16)


def solution(mesh):
    placed = (P("tower", "seq", None), P("tower", "seq", None), P("tower", "seq", None), P(), P())
    return jax.shard_map(
        local, mesh=mesh, in_specs=placed, out_specs=P("tower", "seq", None), check_vma=False
    )
```

profile of v0, /device:TPU:7, one launch (start us, length us, event | category | flops | bytes accessed | tf_op | source)
XLA Modules:
  0.0 233.7 jit_solution(7783236076697758818)
XLA Ops:
  6.5 0.0 all-gather.5.cloned.1.call-start
  6.5 0.7 all-gather.5.cloned.1.call-update
  7.3 0.0 all-gather.3.cloned.1.call-start
  7.3 0.7 all-gather.3.cloned.1.call-update
  8.0 44.2 %all-gather.5.cloned.1.call-done = bf16[4,128,3072]{2,1,0:T(8,128)(2,1)} async-done(((bf16[1,128,3072]{2,1,0:T(8,128)(2,1)}), bf16[4,128,3072]{2,1,0:T(8,128)(2,1)}) %all-gather.5.cloned.1.call-update) | async-done | bytes 3145744 | tf_op jit(solution)/shard_map/all_gather | solution.py:69
  52.2 2.5 %slice_bitcast_fusion.18 = (bf16[128,3072]{1,0:T(8,128)(2,1)}, bf16[1,128,3072]{2,1,0:T(8,128)(2,1)S(1)}, bf16[1,128,3072]{2,1,0:T(8,128)(2,1)S(1)}) fusion(bf16[4,128,3072]{2,1,0:T(8,128)(2,1)} %all-gather.5.cloned.1.call-done), kind=kLoop, calls=%fused_computation.80 | loop fusion | bytes 3932160 | tf_op jit(solution)/shard_map/squeeze | solution.py:94
  54.8 40.5 %all-gather.3.cloned.1.call-done = bf16[4,128,3072]{2,1,0:T(8,128)(2,1)} async-done(((bf16[1,128,3072]{2,1,0:T(8,128)(2,1)}), bf16[4,128,3072]{2,1,0:T(8,128)(2,1)}) %all-gather.3.cloned.1.call-update) | async-done | bytes 3145744 | tf_op jit(solution)/shard_map/all_gather | solution.py:68
  95.3 2.5 %slice_bitcast_fusion.19 = (bf16[128,3072]{1,0:T(8,128)(2,1)}, bf16[1,128,3072]{2,1,0:T(8,128)(2,1)S(1)}, bf16[1,128,3072]{2,1,0:T(8,128)(2,1)S(1)}) fusion(bf16[4,128,3072]{2,1,0:T(8,128)(2,1)} %all-gather.3.cloned.1.call-done), kind=kLoop, calls=%fused_computation.81 | loop fusion | bytes 3932160 | tf_op jit(solution)/shard_map/squeeze | solution.py:93
  97.8 0.3 maximum_bitcast_fusion
  98.0 0.0 copy-start.1
  98.0 0.0 copy-start.2
  98.1 1.9 pad_maximum_fusion.1
  100.0 8.0 %collective-permute-start.1 = (bf16[2,2,128,3072]{3,2,1,0:T(8,128)(2,1)}, bf16[2,2,128,3072]{3,2,1,0:T(8,128)(2,1)}, u32[]{:S(2)}, u32[]{:S(2)}) collective-permute-start(bf16[2,2,128,3072]{3,2,1,0:T(8,128)(2,1)} %pad_maximum_fusion.1), channel_id=1, source_target_pairs={{1,0},{2,1},{3,2},{4,3},{5,4},{6,5},{7,6},{8,7},{9,8},{10,9},{11,1... | collective-permute-start | bytes 9437192 | tf_op jit(solution)/shard_map/ppermute | solution.py:14
  107.9 0.0 copy-done.1
  107.9 0.1 slice_bitcast_fusion.2
  108.1 0.0 copy-done.2
  108.1 0.1 slice_bitcast_fusion.3
  108.2 0.0 copy-start.9
  108.2 2.0 pad_maximum_fusion
  110.1 1.9 collective-permute-start
  112.1 0.0 copy-done.9
  112.1 0.0 copy-start.7
  112.1 63.8 %collective-permute-done.1 = bf16[2,2,128,3072]{3,2,1,0:T(8,128)(2,1)} collective-permute-done((bf16[2,2,128,3072]{3,2,1,0:T(8,128)(2,1)}, bf16[2,2,128,3072]{3,2,1,0:T(8,128)(2,1)}, u32[]{:S(2)}, u32[]{:S(2)}) %collective-permute-start.1) | collective-permute-done | bytes 3145760 | tf_op jit(solution)/shard_map/ppermute | solution.py:14
  176.0 1.5 slice_bitcast_fusion.12
  177.4 0.0 copy-start.8
  177.4 10.3 %collective-permute-done = bf16[2,2,128,3072]{3,2,1,0:T(8,128)(2,1)} collective-permute-done((bf16[2,2,128,3072]{3,2,1,0:T(8,128)(2,1)}, bf16[2,2,128,3072]{3,2,1,0:T(8,128)(2,1)}, u32[]{:S(2)}, u32[]{:S(2)}) %collective-permute-start) | collective-permute-done | bytes 3145760 | tf_op jit(solution)/shard_map/ppermute | solution.py:14
  187.7 1.5 slice_bitcast_fusion.13
  189.2 0.0 copy-done.7
  189.2 1.6 pad_maximum_fusion.3
  190.8 0.0 copy-done.8
  190.8 0.0 copy-start.3
  190.8 1.6 pad_maximum_fusion.2
  192.4 2.8 %fusion.39 = (bf16[640,3072]{1,0:T(8,128)(2,1)}, bf16[640,3072]{1,0:T(8,128)(2,1)}) fusion(bf16[2,2,128,3072]{3,2,1,0:T(8,128)(2,1)} %collective-permute-done), kind=kLoop, calls=%fused_computation.63 | loop fusion | bytes 3145728
  195.2 0.0 copy-done.3
  195.2 1.2 bitcast_dynamic-update-slice_fusion
  196.4 0.9 fusion.38
  197.4 0.0 copy-start.10
  197.4 1.0 fusion.37
  198.3 0.0 copy-start.4
  198.3 0.0 copy-start.6
  198.3 0.9 fusion.42
  199.3 1.0 fusion.41
  200.2 2.6 %fusion.36 = (bf16[640,3072]{1,0:T(8,128)(2,1)}, bf16[640,3072]{1,0:T(8,128)(2,1)}) fusion(bf16[640,3072]{1,0:T(8,128)(2,1)} %fusion.37, bf16[2,2,128,3072]{3,2,1,0:T(8,128)(2,1)} %collective-permute-done.1, bf16[640,3072]{1,0:T(8,128)(2,1)} %fusion.41), kind=kLoop, calls=%fused_computation.57 | loop fusion | bytes 3145728 | tf_op jit(solution)/shard_map/concatenate | solution.py:90
  202.8 0.0 copy-done.10
  202.8 0.0 copy-done.4
  202.8 0.0 copy-done.6
  202.8 22.9 %conditional.6 = (bf16[1,128,3072]{1,2,0:T(8,128)(2,1)S(1)}) conditional(s32[]{:T(128)} %convert_element_type.28, (s32[]{:T(128)}, s32[]{:T(128)}, s32[64]{0:T(128)S(1)}, s32[64]{0:T(128)S(1)}, bf16[1,128,3072]{2,1,0:T(8,128)(2,1)S(1)}, /*index=5*/bf16[384,3072]{1,0:T(8,128)(2,1)}, bf16[384,3072]{1,0:T(8,128)(2,1)S(1)}, ...), branch_computations={%region_0.4_spmd, %region_3.7_spmd} | conditional | flops 1029433408 | bytes 73989080
  203.0 0.6 dynamic-slice.4
  204.3 0.6 dynamic-slice.5
  205.4 0.1 broadcast_bitcast_fusion
  205.5 0.2 copy.32
  205.7 3.8 %fusion = (f32[24,128]{1,0:T(8,128)S(1)}, f32[24,128,640]{2,1,0:T(8,128)S(1)}) fusion(pred[640]{0:T(1024)(128)(4,1)S(1)} %broadcast_bitcast_fusion, bf16[128,24,128]{2,1,0:T(8,128)(2,1)S(1)} %bitcast.114, bf16[640,3072]{1,0:T(8,128)(2,1)} %get-tuple-element.114), kind=kOutput, calls=%fused_computation.4 | convolution fusion | flops 509211648 | bytes 12595840 | tf_op jit(solution)/shard_map/cond/branch_1_fun/while/body/eval_jaxpr/qhd,khd->hqk/dot_general | solution.py:23
  209.5 0.0 copy-start
  209.5 2.0 fusion.1
  211.5 1.2 copy-done
  212.7 6.2 %copy.29 = bf16[640,3072]{0,1:T(8,128)(2,1)} copy(bf16[640,3072]{1,0:T(8,128)(2,1)} %get-tuple-element.182) | data formatting | bytes 7864320 | tf_op jit(solution)/shard_map
  218.8 6.9 %fusion.12 = bf16[128,24,128]{0,2,1:T(8,128)(2,1)S(1)} fusion(bf16[640,24,128]{0,2,1:T(8,128)(2,1)} %bitcast.111, f32[24,128,640]{2,1,0:T(8,128)} %copy-done, f32[24,128]{1,0:T(8,128)S(1)} %get-tuple-element.184, pred[640]{0:T(1024)(128)(4,1)S(1)} %broadcast_bitcast_fusion, f32[24]{0:T(128)S(1)} %slice_bitcast_fusion, f32[128,24]{0,1:T(8,128)S(1)} %bitcast.120), kind=kOutput, calls=%fused_computation.16 | convolution fusion | flops 512360448 | bytes 12608224 | tf_op jit(solution)/shard_map/cond/branch_1_fun/while/body/eval_jaxpr/hqk,khd->qhd/dot_general | solution.py:31
  225.7 1.2 copy.30
  (3 shorter events, 0.0 us)
Async XLA Ops:
  6.5 45.7 %all-gather.5.cloned.1.call-start = ((), (), s32[]{:S(2)}) async-start(), calls=%async_computation.1 | async-start | bytes 3932160 | tf_op jit(solution)/shard_map/all_gather | solution.py:69
  7.3 88.0 %all-gather.3.cloned.1.call-start = ((), (), s32[]{:S(2)}) async-start(), calls=%async_computation | async-start | bytes 3932160 | tf_op jit(solution)/shard_map/all_gather | solution.py:68
  98.0 9.9 %copy-start.1 = (bf16[4,128,3072]{2,1,0:T(8,128)(2,1)S(1)}, bf16[4,128,3072]{2,1,0:T(8,128)(2,1)}, u32[]{:S(2)}) copy-start(bf16[4,128,3072]{2,1,0:T(8,128)(2,1)} %all-gather.5.cloned.1.call-done) | copy-start | bytes 9437188
  98.0 10.0 %copy-start.2 = (bf16[4,128,3072]{2,1,0:T(8,128)(2,1)S(1)}, bf16[4,128,3072]{2,1,0:T(8,128)(2,1)}, u32[]{:S(2)}) copy-start(bf16[4,128,3072]{2,1,0:T(8,128)(2,1)} %all-gather.3.cloned.1.call-done) | copy-start | bytes 9437188
  100.0 76.0 %collective-permute-start.1 = (bf16[2,2,128,3072]{3,2,1,0:T(8,128)(2,1)}, bf16[2,2,128,3072]{3,2,1,0:T(8,128)(2,1)}, u32[]{:S(2)}, u32[]{:S(2)}) collective-permute-start(bf16[2,2,128,3072]{3,2,1,0:T(8,128)(2,1)} %pad_maximum_fusion.1), channel_id=1, source_target_pairs={{1,0},{2,1},{3,2},{4,3},{5,4},{6,5},{7,6},{8,7},{9,8},{10,9},{11,1... | collective-permute-start | bytes 9437192 | tf_op jit(solution)/shard_map/ppermute | solution.py:14
  108.2 3.9 %copy-start.9 = (s32[64,2]{0,1:T(2,128)S(1)}, s32[64,2]{0,1:T(2,128)}, u32[]{:S(2)}) copy-start(s32[64,2]{0,1:T(2,128)} %param.12) | copy-start | bytes 1540
  110.1 77.6 %collective-permute-start = (bf16[2,2,128,3072]{3,2,1,0:T(8,128)(2,1)}, bf16[2,2,128,3072]{3,2,1,0:T(8,128)(2,1)}, u32[]{:S(2)}, u32[]{:S(2)}) collective-permute-start(bf16[2,2,128,3072]{3,2,1,0:T(8,128)(2,1)} %pad_maximum_fusion), channel_id=1, source_target_pairs={{0,1},{1,2},{2,3},{3,4},{4,5},{5,6},{6,7},{7,8},{8,9},{9,10},{10,1... | collective-permute-start | bytes 9437192 | tf_op jit(solution)/shard_map/ppermute | solution.py:14
  112.1 77.1 %copy-start.7 = (bf16[128,3072]{1,0:T(8,128)(2,1)S(1)}, bf16[128,3072]{1,0:T(8,128)(2,1)}, u32[]{:S(2)}) copy-start(bf16[128,3072]{1,0:T(8,128)(2,1)} %get-tuple-element.194) | copy-start | bytes 2359300
  177.4 13.3 %copy-start.8 = (bf16[128,3072]{1,0:T(8,128)(2,1)S(1)}, bf16[128,3072]{1,0:T(8,128)(2,1)}, u32[]{:S(2)}) copy-start(bf16[128,3072]{1,0:T(8,128)(2,1)} %get-tuple-element.199) | copy-start | bytes 2359300
  190.8 4.4 %copy-start.3 = (bf16[4,128,3072]{2,1,0:T(8,128)(2,1)S(1)}, bf16[4,128,3072]{2,1,0:T(8,128)(2,1)}, u32[]{:S(2)}) copy-start(bf16[4,128,3072]{2,1,0:T(8,128)(2,1)} %all-gather.3.cloned.1.call-done) | copy-start | bytes 9437188
  197.4 5.5 %copy-start.10 = (f32[2,24]{1,0:T(2,128)S(1)}, f32[2,24]{1,0:T(2,128)}, u32[]{:S(2)}) copy-start(f32[2,24]{1,0:T(2,128)} %param.13) | copy-start | bytes 580
  198.3 4.5 %copy-start.4 = (bf16[384,3072]{1,0:T(8,128)(2,1)S(1)}, bf16[384,3072]{1,0:T(8,128)(2,1)}, u32[]{:S(2)}) copy-start(bf16[384,3072]{1,0:T(8,128)(2,1)} %pad_maximum_fusion.3) | copy-start | bytes 7077892
  198.3 4.5 %copy-start.6 = (bf16[1,128,3072]{2,1,0:T(8,128)(2,1)S(1)}, bf16[1,128,3072]{2,1,0:T(8,128)(2,1)}, u32[]{:S(2)}) copy-start(bf16[1,128,3072]{2,1,0:T(8,128)(2,1)} %param.9) | copy-start | bytes 2359300
  209.5 3.1 %copy-start = (f32[24,128,640]{2,1,0:T(8,128)}, f32[24,128,640]{2,1,0:T(8,128)S(1)}, u32[]{:S(2)}) copy-start(f32[24,128,640]{2,1,0:T(8,128)S(1)} %get-tuple-element.185) | copy-start | bytes 23592964 | tf_op jit(solution)/shard_map/conditional.1
Sparse Core Ops, SparseCore 0:
  9.1 43.0 all-gather.4
  54.0 41.2 all-gather.2
where the time goes:
time: 234 us
  waiting for transfers between devices  160 us (68%)
  local copies, waits for them, and re-layouts  28.5 us (12%)
  between operations  13.5 us (6%)
  matrix products  10.7 us (5%)
  starting transfers between devices  9.92 us (4%)
  other arithmetic  9.3 us (4%)
    ppermute x2, waiting for transfers between devices, from_behind(): return lax.ppermute(block, axis, route)  74.1 us
    all_gather x1, waiting for transfers between devices, local(): lax.all_gather(values, 'tower', axis=0, tiled=True)  44.2 us
    all_gather x1, waiting for transfers between devices, local(): lax.all_gather(keys, 'tower', axis=0, tiled=True)  40.5 us
    ppermute x2, starting transfers between devices, from_behind(): return lax.ppermute(block, axis, route)  9.87 us
    unnamed x24, local copies, waits for them, and re-layouts  7.85 us
    another operation x4, local copies, waits for them, and re-layouts  7.48 us
    dot_general x1, matrix products, attend(): jnp.einsum('hqk,khd->qhd', rounded, v_heads, preferred_element_type=jnp.f...  6.88 us
  transfers between devices with their start and end apart: 4, of which 4 were waited for; matrix products, arithmetic and copies ran while one was open for 3% of the time, Pallas kernels for 0%

commit v1 on v0

v1 whole, which is shorter than its diff:
```python
import functools
import math

import jax
import jax.numpy as jnp
from jax import lax
from jax.experimental import pallas as pl
from jax.experimental.pallas import tpu as pltpu
from jax.sharding import PartitionSpec as P

HEADS = 24
DIM = 128
BLOCK = 128
WIDTH = HEADS * DIM
PER = 2
CHUNKS = HEADS // PER
HALF = CHUNKS // 2
SPAN = PER * DIM
COLD = math.log2(math.e) / math.sqrt(DIM)
MESH = pl.DeviceIdType.MESH


def cols(chunk):
    return pl.ds(pl.multiple_of(chunk * SPAN, SPAN), SPAN)


def head_cols(head):
    return pl.ds(pl.multiple_of(head * DIM, DIM), DIM)


def loop(count, body):
    def step(i, carry):
        body(i)
        return carry

    lax.fori_loop(0, count, step, 0)


def mix(q, k, v, bias):
    scores = lax.dot_general(q, k, (((1,), (1,)), ((), ())), preferred_element_type=jnp.float32)
    if bias is not None:
        scores = scores + bias
    top = jnp.max(scores, axis=1, keepdims=True)
    weights = jnp.exp2((scores - top) * COLD)
    total = jnp.sum(weights, axis=1, keepdims=True)
    mixed = jnp.dot(weights.astype(jnp.bfloat16), v, preferred_element_type=jnp.float32)
    return mixed, top, total


def bias_row(linked, blocks):
    off = jnp.where(linked, 0.0, -jnp.inf).astype(jnp.float32)
    place = lax.broadcasted_iota(jnp.int32, (1, blocks * BLOCK), 1)
    return jnp.where(place >= (blocks - 1) * BLOCK, off, 0.0)


def kernel(
    seq_count,
    align_ref,
    gate_ref,
    q_hbm,
    k_hbm,
    v_hbm,
    out_hbm,
    q_own,
    main_k,
    main_v,
    aud_q,
    aud_k,
    aud_v,
    part_out,
    part_stat,
    part_in,
    stat_in,
    local_mix,
    local_top,
    local_total,
    out_buf,
    local_sem,
    out_sem,
    send_a,
    send_b,
    send_c,
    send_d,
    recv_near,
    recv_next,
    recv_q,
    recv_pair,
    recv_third,
    recv_part,
    recv_stat,
):
    tower = lax.axis_index("tower")
    column = lax.axis_index("seq")
    is_first = column == 0
    is_last = column == seq_count - 1
    before = jnp.maximum(column - 1, 0)
    after = jnp.minimum(column + 1, seq_count - 1)
    sources = (k_hbm, v_hbm)
    mains = (main_k, main_v)
    auds = (aud_k, aud_v)

    def device(t, c):
        return {"tower": t, "seq": c}

    def remote(src, dst, send, recv, t, c):
        return pltpu.make_async_remote_copy(
            src_ref=src, dst_ref=dst, send_sem=send, recv_sem=recv, device_id=device(t, c), device_id_type=MESH
        )

    q_copy = pltpu.make_async_copy(q_hbm.at[0], q_own, local_sem.at[2])
    q_copy.start()

    barrier = pltpu.get_barrier_semaphore()

    def greet(t, c):
        pl.semaphore_signal(barrier, inc=1, device_id=device(t, c), device_id_type=MESH)

    def meet(fixed, backward, forward):
        for t in fixed:
            greet(t, column)

        @pl.when(jnp.logical_not(is_first))
        def _():
            for t in backward:
                greet(t, before)

        @pl.when(jnp.logical_not(is_last))
        def _():
            for t in forward:
                greet(t, after)

        peers = jnp.int32(len(fixed))
        peers = peers + jnp.where(is_first, 0, len(backward))
        peers = peers + jnp.where(is_last, 0, len(forward))
        pl.semaphore_wait(barrier, peers)

    @pl.when(tower == 0)
    def _():
        meet((1, 3), (0, 1), (0,))

    @pl.when(tower == 1)
    def _():
        meet((0, 3), (), (0,))

    @pl.when(tower == 2)
    def _():
        meet((3,), (), (3,))

    @pl.when(tower == 3)
    def _():
        meet((0, 1, 2), (2,), ())

    near_rows = pl.ds(0, BLOCK)
    next_rows = pl.ds(BLOCK, BLOCK)
    third_rows = pl.ds(2 * BLOCK, BLOCK)

    def write_out(chunk):
        return pltpu.make_async_copy(
            out_buf.at[:, cols(chunk)], out_hbm.at[0, :, cols(chunk)], out_sem.at[chunk]
        )

    def recv_main(which, chunk, rows, sems):
        dst = mains[which].at[rows, cols(chunk)]
        return remote(dst, dst, send_a.at[which, chunk], sems.at[which, chunk], tower, column)

    def await_near(chunk):
        for which in range(2):
            recv_main(which, chunk, near_rows, recv_near).wait_recv()

    def await_next(chunk):
        for which in range(2):
            recv_main(which, chunk, next_rows, recv_next).wait_recv()

    def video_heads(chunk, blocks, bias):
        for i in range(PER):
            head = chunk * PER + i
            at = head_cols(head)
            mixed, _, total = mix(
                q_own[:, at], main_k[0 : blocks * BLOCK, at], main_v[0 : blocks * BLOCK, at], bias
            )
            out_buf[:, at] = (mixed * (gate_ref[0, head] / total)).astype(jnp.bfloat16)
        write_out(chunk).start()

    def finish_out(chunk):
        write_out(chunk).wait()

    @pl.when(tower < 2)
    def _():
        other = 1 - tower
        own_base = tower * HALF
        other_base = other * HALF
        own_rows = pl.ds(pl.multiple_of(tower * BLOCK, BLOCK), BLOCK)
        half_cols = pl.ds(pl.multiple_of(own_base * SPAN, SPAN), HALF * SPAN)
        other_cols = pl.ds(pl.multiple_of(other_base * SPAN, SPAN), HALF * SPAN)
        pair_rows = pl.ds(pl.multiple_of(other * BLOCK, BLOCK), BLOCK)

        def own_copy(which):
            return pltpu.make_async_copy(
                sources[which].at[0, :, half_cols], auds[which].at[own_rows, :], local_sem.at[which]
            )

        def pair_copy(which):
            return remote(
                sources[which].at[0, :, other_cols],
                auds[which].at[own_rows, :],
                send_c.at[which, 0],
                recv_pair.at[which],
                other,
                column,
            )

        def pair_wait(which):
            dst = auds[which].at[pair_rows, :]
            return remote(dst, dst, send_c.at[which, 0], recv_pair.at[which], tower, column)

        def third_copy(which, half, chunk):
            src = sources[which].at[0, :, cols(half * HALF + chunk)]
            dst = auds[which].at[third_rows, cols(chunk)]
            return remote(
                src, dst, send_d.at[which, half * HALF + chunk], recv_third.at[which, chunk], half, before
            )

        def third_wait(which, chunk):
            dst = auds[which].at[third_rows, cols(chunk)]
            return remote(dst, dst, send_d.at[which, chunk], recv_third.at[which, chunk], tower, column)

        def pass_pair(which, chunk):
            part = mains[which].at[near_rows, cols(chunk)]
            return remote(part, part, send_a.at[which, chunk], recv_near.at[which, chunk], other, column)

        def pass_next(which, chunk):
            return remote(
                mains[which].at[near_rows, cols(chunk)],
                mains[which].at[next_rows, cols(chunk)],
                send_b.at[which, chunk],
                recv_next.at[which, chunk],
                0,
                after,
            )

        def part_copy(chunk):
            return remote(
                part_out.at[:, cols(chunk)],
                part_in.at[:, cols(own_base + chunk)],
                send_c.at[0, 1 + chunk],
                recv_part.at[own_base + chunk],
                3,
                column,
            )

        def stat_copy(chunk):
            return remote(
                part_stat.at[chunk],
                stat_in.at[own_base + chunk],
                send_c.at[1, 1 + chunk],
                recv_stat.at[own_base + chunk],
                3,
                column,
            )

        for which in range(2):
            pair_copy(which).start()

        @pl.when(jnp.logical_and(tower == 0, jnp.logical_not(is_first)))
        def _():
            def start(chunk):
                for half in range(2):
                    for which in range(2):
                        third_copy(which, half, chunk).start()

            loop(HALF, start)

        for which in range(2):
            own_copy(which).start()

        @pl.when(jnp.logical_and(tower == 0, is_first))
        def _():
            for ref in mains:
                ref[BLOCK : 2 * BLOCK, :] = jnp.zeros((BLOCK, WIDTH), jnp.bfloat16)

        @pl.when(is_last)
        def _():
            for ref in auds:
                ref[2 * BLOCK : 3 * BLOCK, :] = jnp.zeros((BLOCK, WIDTH // 2), jnp.bfloat16)

        q_copy.wait()
        video_bias = bias_row(jnp.logical_and(column > 0, align_ref[before, 1] > 3 * column), 2)
        audio_bias = bias_row(align_ref[column, 1] > 3 * column + 3, 3)

        def video(step):
            @pl.when(tower == 0)
            def _():
                for base in (0, HALF):
                    chunk = base + step

                    @pl.when(jnp.logical_not(is_first))
                    def _():
                        await_next(chunk)

            await_near(other_base + step)

            @pl.when(tower == 0)
            def _():
                for base in (0, HALF):
                    video_heads(base + step, 2, video_bias)

            @pl.when(tower == 1)
            def _():
                for base in (0, HALF):
                    video_heads(base + step, 1, None)

        def take(step):
            chunk = own_base + step
            await_near(chunk)
            for which in range(2):
                pass_pair(which, chunk).start()

            @pl.when(jnp.logical_not(is_last))
            def _():
                for which in range(2):
                    pass_next(which, chunk).start()

            @pl.when(step > 0)
            def _():
                video(step - 1)

        loop(HALF, take)
        video(HALF - 1)

        for which in range(2):
            own_copy(which).wait()
            pair_wait(which).wait_recv()

        def audio(step):
            dst = aud_q.at[:, cols(step)]
            remote(dst, dst, send_a.at[0, step], recv_q.at[step], tower, column).wait_recv()

            @pl.when(jnp.logical_not(is_last))
            def _():
                for which in range(2):
                    third_wait(which, step).wait_recv()

            lane = lax.broadcasted_iota(jnp.int32, (BLOCK, DIM), 1)
            stat = jnp.zeros((BLOCK, DIM), jnp.float32)
            for i in range(PER):
                at = head_cols(step * PER + i)
                mixed, top, total = mix(aud_q[:, at], aud_k[:, at], aud_v[:, at], audio_bias)
                part_out[:, at] = mixed.astype(jnp.bfloat16)
                stat = jnp.where(lane == 2 * i, top, stat)
                stat = jnp.where(lane == 2 * i + 1, total, stat)
            part_stat[step] = jnp.transpose(stat)[0:8]
            stat_copy(step).start()
            part_copy(step).start()

        loop(HALF, audio)

        for which in range(2):
            pair_copy(which).wait_send()

        @pl.when(jnp.logical_and(tower == 0, jnp.logical_not(is_first)))
        def _():
            def drain(chunk):
                for half in range(2):
                    for which in range(2):
                        third_copy(which, half, chunk).wait_send()

            loop(HALF, drain)

        def drain(step):
            chunk = own_base + step
            for which in range(2):
                pass_pair(which, chunk).wait_send()

            @pl.when(jnp.logical_not(is_last))
            def _():
                for which in range(2):
                    pass_next(which, chunk).wait_send()

            stat_copy(step).wait_send()
            part_copy(step).wait_send()

        loop(HALF, drain)
        loop(CHUNKS, finish_out)

    @pl.when(tower == 2)
    def _():
        def near_copy(which, chunk):
            return remote(
                sources[which].at[0, :, cols(chunk)],
                mains[which].at[near_rows, cols(chunk)],
                send_a.at[which, chunk],
                recv_near.at[which, chunk],
                3,
                column,
            )

        def next_copy(which, chunk):
            return remote(
                sources[which].at[0, :, cols(chunk)],
                mains[which].at[next_rows, cols(chunk)],
                send_b.at[which, chunk],
                recv_next.at[which, chunk],
                3,
                after,
            )

        def start_near(chunk):
            for which in range(2):
                near_copy(which, chunk).start()

        def start_next(chunk):
            for which in range(2):
                next_copy(which, chunk).start()

        @pl.when(jnp.logical_not(is_last))
        def _():
            loop(CHUNKS, start_next)

        loop(CHUNKS, start_near)

        @pl.when(is_last)
        def _():
            for ref in mains:
                ref[BLOCK : 2 * BLOCK, :] = jnp.zeros((BLOCK, WIDTH), jnp.bfloat16)

        q_copy.wait()
        linked = jnp.logical_and(column < seq_count - 1, align_ref[after, 0] <= 3 * column + 2)
        bias = bias_row(linked, 2)

        def video(chunk):
            await_near(chunk)

            @pl.when(jnp.logical_not(is_last))
            def _():
                await_next(chunk)

            video_heads(chunk, 2, bias)

        loop(CHUNKS, video)

        def drain(chunk):
            for which in range(2):
                near_copy(which, chunk).wait_send()

            @pl.when(jnp.logical_not(is_last))
            def _():
                for which in range(2):
                    next_copy(which, chunk).wait_send()

            finish_out(chunk)

        loop(CHUNKS, drain)

    @pl.when(tower == 3)
    def _():
        def far_copy(which, half, step):
            chunk = half * HALF + step
            return remote(
                sources[which].at[0, :, cols(chunk)],
                mains[which].at[near_rows, cols(chunk)],
                send_a.at[which, chunk],
                recv_near.at[which, chunk],
                half,
                column,
            )

        def query_copy(half, step):
            return remote(
                q_hbm.at[0, :, cols(half * HALF + step)],
                aud_q.at[:, cols(step)],
                send_d.at[half, step],
                recv_q.at[step],
                half,
                column,
            )

        def near_copy(which, chunk):
            return remote(
                sources[which].at[0, :, cols(chunk)],
                mains[which].at[near_rows, cols(chunk)],
                send_b.at[which, chunk],
                recv_near.at[which, chunk],
                2,
                column,
            )

        def back_copy(which, chunk):
            return remote(
                sources[which].at[0, :, cols(chunk)],
                mains[which].at[next_rows, cols(chunk)],
                send_c.at[which, chunk],
                recv_next.at[which, chunk],
                2,
                before,
            )

        def start_far(step):
            for half in range(2):
                for which in range(2):
                    far_copy(which, half, step).start()

        loop(HALF, start_far)

        def start_query(step):
            for half in range(2):
                query_copy(half, step).start()

        loop(HALF, start_query)

        @pl.when(jnp.logical_not(is_first))
        def _():
            def start_back(chunk):
                for which in range(2):
                    back_copy(which, chunk).start()

            loop(CHUNKS, start_back)

        def start_near(chunk):
            for which in range(2):
                near_copy(which, chunk).start()

        loop(CHUNKS, start_near)

        @pl.when(is_first)
        def _():
            for ref in mains:
                ref[BLOCK : 2 * BLOCK, :] = jnp.zeros((BLOCK, WIDTH), jnp.bfloat16)

        q_copy.wait()
        bias = bias_row(align_ref[column, 0] <= 3 * column - 1, 2)

        def local(chunk):
            await_near(chunk)

            @pl.when(jnp.logical_not(is_first))
            def _():
                await_next(chunk)

            for i in range(PER):
                head = chunk * PER + i
                at = head_cols(head)
                mixed, top, total = mix(q_own[:, at], main_k[:, at], main_v[:, at], bias)
                local_mix[:, at] = mixed
                local_top[head] = jnp.broadcast_to(top, (BLOCK, DIM))
                local_total[head] = jnp.broadcast_to(total, (BLOCK, DIM))

        loop(CHUNKS, local)

        def merge_chunk(chunk):
            dst = stat_in.at[chunk]
            remote(dst, dst, send_a.at[0, chunk], recv_stat.at[chunk], tower, column).wait_recv()
            dst = part_in.at[:, cols(chunk)]
            remote(dst, dst, send_a.at[0, chunk], recv_part.at[chunk], tower, column).wait_recv()
            stat = jnp.concatenate([stat_in[chunk], jnp.zeros((DIM - 8, BLOCK), jnp.float32)], axis=0)
            stat = jnp.transpose(stat)
            for i in range(PER):
                head = chunk * PER + i
                at = head_cols(head)
                far_top = stat[:, 2 * i : 2 * i + 1]
                far_total = stat[:, 2 * i + 1 : 2 * i + 2]
                near_top = local_top[head][:, 0:1]
                near_total = local_total[head][:, 0:1]
                top = jnp.maximum(far_top, near_top)
                far = jnp.exp2((far_top - top) * COLD)
                near = jnp.exp2((near_top - top) * COLD)
                scale = gate_ref[1, head] / (far * far_total + near * near_total)
                mixed = part_in[:, at].astype(jnp.float32) * (far * scale) + local_mix[:, at] * (near * scale)
                out_buf[:, at] = mixed.astype(jnp.bfloat16)
            write_out(chunk).start()

        def merge(step):
            for half in range(2):
                merge_chunk(half * HALF + step)

        loop(HALF, merge)

        def drain_far(step):
            for half in range(2):
                for which in range(2):
                    far_copy(which, half, step).wait_send()
                query_copy(half, step).wait_send()

        loop(HALF, drain_far)

        def drain(chunk):
            for which in range(2):
                near_copy(which, chunk).wait_send()

            @pl.when(jnp.logical_not(is_first))
            def _():
                for which in range(2):
                    back_copy(which, chunk).wait_send()

            finish_out(chunk)

        loop(CHUNKS, drain)


def local(seq_count, queries, keys, values, alignment, cross_gate):
    bf16, f32 = jnp.bfloat16, jnp.float32
    dma = pltpu.SemaphoreType.DMA
    any_space = pl.BlockSpec(memory_space=pl.ANY)
    smem = pl.BlockSpec(memory_space=pltpu.SMEM)
    return pl.pallas_call(
        functools.partial(kernel, seq_count),
        out_shape=jax.ShapeDtypeStruct(queries.shape, bf16),
        in_specs=[smem, smem, any_space, any_space, any_space],
        out_specs=any_space,
        scratch_shapes=[
            pltpu.VMEM((BLOCK, WIDTH), bf16),
            pltpu.VMEM((2 * BLOCK, WIDTH), bf16),
            pltpu.VMEM((2 * BLOCK, WIDTH), bf16),
            pltpu.VMEM((BLOCK, WIDTH // 2), bf16),
            pltpu.VMEM((3 * BLOCK, WIDTH // 2), bf16),
            pltpu.VMEM((3 * BLOCK, WIDTH // 2), bf16),
            pltpu.VMEM((BLOCK, WIDTH // 2), bf16),
            pltpu.VMEM((HALF, 8, BLOCK), f32),
            pltpu.VMEM((BLOCK, WIDTH), bf16),
            pltpu.VMEM((CHUNKS, 8, BLOCK), f32),
            pltpu.VMEM((BLOCK, WIDTH), f32),
            pltpu.VMEM((HEADS, BLOCK, DIM), f32),
            pltpu.VMEM((HEADS, BLOCK, DIM), f32),
            pltpu.VMEM((BLOCK, WIDTH), bf16),
            dma((3,)),
            dma((CHUNKS,)),
            dma((2, CHUNKS)),
            dma((2, CHUNKS)),
            dma((2, CHUNKS)),
            dma((2, CHUNKS)),
            dma((2, CHUNKS)),
            dma((2, CHUNKS)),
            dma((HALF,)),
            dma((2,)),
            dma((2, HALF)),
            dma((CHUNKS,)),
            dma((CHUNKS,)),
        ],
        compiler_params=pltpu.CompilerParams(
            collective_id=0, has_side_effects=True, vmem_limit_bytes=48 * 1024 * 1024
        ),
    )(alignment, cross_gate, queries, keys, values)


def solution(mesh):
    placed = (P("tower", "seq", None), P("tower", "seq", None), P("tower", "seq", None), P(), P())
    return jax.shard_map(
        functools.partial(local, mesh.shape["seq"]),
        mesh=mesh,
        in_specs=placed,
        out_specs=P("tower", "seq", None),
        check_vma=False,
    )
```

time: 234 us -> 62.6 us (0.27)
  the two profiles are of different devices: /device:TPU:7 before, /device:TPU:239 now
where the time goes in v1:
time: 62.6 us; the launch traced here: 62.4 us
  Pallas kernels  57.3 us (92%)
  local copies, waits for them, and re-layouts  5.06 us (8%)
    pallas_call x1, Pallas kernels, local(): pl.pallas_call(functools.partial(kernel, seq_count), out_shape=jax.ShapeD...  57.3 us
    unnamed x10, local copies, waits for them, and re-layouts  5.06 us

profile of v1, /device:TPU:239, one launch (start us, length us, event | category | flops | bytes accessed | tf_op | source)
XLA Modules:
  0.0 62.4 jit_solution(16069305726863119993)
XLA Ops:
  0.0 0.0 copy-start.3
  0.0 0.8 %copy.6.align_ref = s32[64,2]{1,0:T(8,128)S(1)} copy(s32[64,2]{0,1:T(2,128)} %param.8) | data formatting | bytes 1024 | tf_op args[3]
  0.8 0.0 copy-done.3
  0.8 0.0 copy-start
  0.8 1.1 %copy-done = bf16[1,128,3072]{2,1,0:T(8,128)(2,1)S(1)} copy-done((bf16[1,128,3072]{2,1,0:T(8,128)(2,1)S(1)}, bf16[1,128,3072]{2,1,0:T(8,128)(2,1)}, u32[]{:S(2)}) %copy-start) | copy-done | bytes 786456
  1.9 0.0 copy-start.1
  1.9 1.1 %copy-done.1 = bf16[1,128,3072]{2,1,0:T(8,128)(2,1)S(1)} copy-done((bf16[1,128,3072]{2,1,0:T(8,128)(2,1)S(1)}, bf16[1,128,3072]{2,1,0:T(8,128)(2,1)}, u32[]{:S(2)}) %copy-start.1) | copy-done | bytes 786456
  3.1 0.0 copy-start.2
  3.1 1.1 %copy-done.2 = bf16[1,128,3072]{2,1,0:T(8,128)(2,1)S(1)} copy-done((bf16[1,128,3072]{2,1,0:T(8,128)(2,1)S(1)}, bf16[1,128,3072]{2,1,0:T(8,128)(2,1)}, u32[]{:S(2)}) %copy-start.2) | copy-done | bytes 786456
  4.2 57.3 %shard_map.55 = bf16[1,128,3072]{2,1,0:T(8,128)(2,1)S(1)} custom-call(s32[64,2]{1,0:T(8,128)S(1)} %copy.6.align_ref, f32[2,24]{1,0:T(2,128)S(1)} %copy-done.3, bf16[1,128,3072]{2,1,0:T(8,128)(2,1)S(1)} %copy-done, bf16[1,128,3072]{2,1,0:T(8,128)(2,1)S(1)} %copy-done.1, bf16[1,128,3072]{2,1,0:T(8,128)(2,1)S(1)} %copy-done.2), custom_call_target="tpu_custom_call" | custom-call | tf_op jit(solution)/shard_map/pallas_call | solution.py:604
  61.5 0.9 %copy.8 = bf16[1,128,3072]{2,1,0:T(8,128)(2,1)} copy(bf16[1,128,3072]{2,1,0:T(8,128)(2,1)S(1)} %shard_map.55) | data formatting | bytes 1572864
Async XLA Ops:
  0.0 0.8 %copy-start.3 = (f32[2,24]{1,0:T(2,128)S(1)}, f32[2,24]{1,0:T(2,128)}, u32[]{:S(2)}) copy-start(f32[2,24]{1,0:T(2,128)} %gate_ref.1) | copy-start | bytes 580
  0.8 1.1 %copy-start = (bf16[1,128,3072]{2,1,0:T(8,128)(2,1)S(1)}, bf16[1,128,3072]{2,1,0:T(8,128)(2,1)}, u32[]{:S(2)}) copy-start(bf16[1,128,3072]{2,1,0:T(8,128)(2,1)} %q_hbm.1) | copy-start | bytes 2359300
  1.9 1.1 %copy-start.1 = (bf16[1,128,3072]{2,1,0:T(8,128)(2,1)S(1)}, bf16[1,128,3072]{2,1,0:T(8,128)(2,1)}, u32[]{:S(2)}) copy-start(bf16[1,128,3072]{2,1,0:T(8,128)(2,1)} %k_hbm.1) | copy-start | bytes 2359300
  3.1 1.1 %copy-start.2 = (bf16[1,128,3072]{2,1,0:T(8,128)(2,1)S(1)}, bf16[1,128,3072]{2,1,0:T(8,128)(2,1)}, u32[]{:S(2)}) copy-start(bf16[1,128,3072]{2,1,0:T(8,128)(2,1)} %v_hbm.1) | copy-start | bytes 2359300

commit v2 on v1

--- a/solution.py
+++ b/solution.py
@@ -55,8 +55,8 @@
 
 def kernel(
     seq_count,
-    align_ref,
-    gate_ref,
+    align_hbm,
+    gate_hbm,
     q_hbm,
     k_hbm,
     v_hbm,
@@ -75,6 +75,17 @@
     local_top,
     local_total,
     out_buf,
+    align_ref,
+    gate_ref,
+    edge_k,
+    edge_v,
+    edge_q,
+    edge_out,
+    edge_stat,
+    edge_in,
+    edge_stat_in,
+    relay_k,
+    relay_v,
     local_sem,
     out_sem,
     send_a,
@@ -88,11 +99,20 @@
     recv_third,
     recv_part,
     recv_stat,
+    send_e,
+    recv_edge_q,
+    recv_edge,
+    recv_edge_stat,
+    recv_relay,
 ):
     tower = lax.axis_index("tower")
     column = lax.axis_index("seq")
     is_first = column == 0
     is_last = column == seq_count - 1
+    edge = seq_count // 2 - 1
+    last = seq_count - 1
+    at_edge = column == edge
+    past_edge = column == edge + 1
     before = jnp.maximum(column - 1, 0)
     after = jnp.minimum(column + 1, seq_count - 1)
     sources = (k_hbm, v_hbm)
@@ -109,50 +129,69 @@
 
     q_copy = pltpu.make_async_copy(q_hbm.at[0], q_own, local_sem.at[2])
     q_copy.start()
+    small = (
+        pltpu.make_async_copy(align_hbm, align_ref, local_sem.at[3]),
+        pltpu.make_async_copy(gate_hbm, gate_ref, local_sem.at[4]),
+    )
+    for copy in small:
+        copy.start()
 
     barrier = pltpu.get_barrier_semaphore()
 
     def greet(t, c):
         pl.semaphore_signal(barrier, inc=1, device_id=device(t, c), device_id_type=MESH)
 
-    def meet(fixed, backward, forward):
+    def meet(fixed, others):
+        peers = jnp.int32(len(fixed))
         for t in fixed:
             greet(t, column)
-
-        @pl.when(jnp.logical_not(is_first))
-        def _():
-            for t in backward:
-                greet(t, before)
-
-        @pl.when(jnp.logical_not(is_last))
-        def _():
-            for t in forward:
-                greet(t, after)
-
-        peers = jnp.int32(len(fixed))
-        peers = peers + jnp.where(is_first, 0, len(backward))
-        peers = peers + jnp.where(is_last, 0, len(forward))
+        for when, t, c in others:
+
+            @pl.when(when)
+            def _():
+                greet(t, c)
+
+            peers = peers + jnp.where(when, 1, 0)
         pl.semaphore_wait(barrier, peers)
+
+    has_back = jnp.logical_not(jnp.logical_or(is_first, past_edge))
+    has_forward = jnp.logical_not(jnp.logical_or(is_last, at_edge))
 
     @pl.when(tower == 0)
     def _():
-        meet((1, 3), (0, 1), (0,))
+        meet(
+            (1, 3),
+            [
+                (has_back, 0, before),
+                (has_back, 1, before),
+                (has_forward, 0, after),
+                (past_edge, 2, edge),
+                (past_edge, 3, edge),
+                (is_last, 2, edge),
+                (is_last, 3, edge + 1),
+            ],
+        )
 
     @pl.when(tower == 1)
     def _():
-        meet((0, 3), (), (0,))
+        meet((0, 3), [(has_forward, 0, after), (past_edge, 2, edge)])
 
     @pl.when(tower == 2)
     def _():
-        meet((3,), (), (3,))
+        meet((3,), [(has_forward, 3, after), (at_edge, 0, edge + 1), (at_edge, 1, edge + 1), (at_edge, 0, last)])
 
     @pl.when(tower == 3)
     def _():
-        meet((0, 1, 2), (2,), ())
+        meet((0, 1, 2), [(has_back, 2, before), (at_edge, 0, edge + 1), (past_edge, 0, last)])
 
     near_rows = pl.ds(0, BLOCK)
     next_rows = pl.ds(BLOCK, BLOCK)
     third_rows = pl.ds(2 * BLOCK, BLOCK)
+
+    def await_own():
+        q_copy.wait()
+        for copy in small:
+            copy.wait()
 
     def write_out(chunk):
         return pltpu.make_async_copy(
@@ -258,10 +297,79 @@
                 column,
             )
 
+        def pass_back(which, chunk):
+            return remote(
+                mains[which].at[near_rows, cols(chunk)],
+                mains[which].at[next_rows, cols(chunk)],
+                send_d.at[which, chunk],
+                recv_next.at[which, chunk],
+                2,
+                before,
+            )
+
+        late = jnp.logical_and(tower == 0, past_edge)
+
+        def edge_own(which):
+            return pltpu.make_async_copy(sources[which].at[0], (edge_k, edge_v)[which], local_sem.at[5 + which])
+
+        def edge_part(chunk):
+            return remote(
+                edge_out.at[:, cols(chunk)], edge_in.at[:, cols(chunk)], send_e.at[0, chunk], recv_edge.at[chunk], 3, edge
+            )
+
+        def edge_stats(chunk):
+            return remote(
+                edge_stat.at[chunk], edge_stat_in.at[chunk], send_e.at[1, chunk], recv_edge_stat.at[chunk], 3, edge
+            )
+
+        def pack(results):
+            lane = lax.broadcasted_iota(jnp.int32, (BLOCK, DIM), 1)
+            stat = jnp.zeros((BLOCK, DIM), jnp.float32)
+            for i, (top, total) in enumerate(results):
+                stat = jnp.where(lane == 2 * i, top, stat)
+                stat = jnp.where(lane == 2 * i + 1, total, stat)
+            return jnp.transpose(stat)[0:8]
+
+        def attend_edge(chunk):
+            dst = edge_q.at[:, cols(chunk)]
+            remote(dst, dst, send_e.at[0, chunk], recv_edge_q.at[chunk], tower, column).wait_recv()
+            results = []
+            for i in range(PER):
+                at = head_cols(chunk * PER + i)
+                mixed, top, total = mix(edge_q[:, at], edge_k[:, at], edge_v[:, at], None)
+                edge_out[:, at] = mixed.astype(jnp.bfloat16)
+                results.append((top, total))
+            edge_stat[chunk] = pack(results)
+            edge_stats(chunk).start()
+            edge_part(chunk).start()
+
+        def relay_copy(which, chunk):
+            return remote(
+                (relay_k, relay_v)[which].at[:, cols(chunk)],
+                mains[which].at[next_rows, cols(chunk)],
+                send_e.at[which, chunk],
+                recv_next.at[which, chunk],
+                3,
+                edge + 1,
+            )
+
+        def relay(chunk):
+            for which in range(2):
+                dst = (relay_k, relay_v)[which].at[:, cols(chunk)]
+                remote(dst, dst, send_e.at[which, chunk], recv_relay.at[which, chunk], tower, column).wait_recv()
+                relay_copy(which, chunk).start()
+
         for which in range(2):
             pair_copy(which).start()
 
-        @pl.when(jnp.logical_and(tower == 0, jnp.logical_not(is_first)))
+        @pl.when(late)
+        def _():
+            for which in range(2):
+                edge_own(which).start()
+            for which in range(2):
+                edge_own(which).wait()
+
+        @pl.when(jnp.logical_and(tower == 0, has_back))
         def _():
             def start(chunk):
                 for half in range(2):
@@ -278,14 +386,14 @@
             for ref in mains:
                 ref[BLOCK : 2 * BLOCK, :] = jnp.zeros((BLOCK, WIDTH), jnp.bfloat16)
 
-        @pl.when(is_last)
+        @pl.when(jnp.logical_not(has_forward))
         def _():
             for ref in auds:
                 ref[2 * BLOCK : 3 * BLOCK, :] = jnp.zeros((BLOCK, WIDTH // 2), jnp.bfloat16)
 
-        q_copy.wait()
-        video_bias = bias_row(jnp.logical_and(column > 0, align_ref[before, 1] > 3 * column), 2)
-        audio_bias = bias_row(align_ref[column, 1] > 3 * column + 3, 3)
+        await_own()
+        video_bias = bias_row(jnp.logical_and(column > 0, align_ref[1, before] > 3 * column), 2)
+        audio_bias = bias_row(jnp.logical_and(has_forward, align_ref[1, column] > 3 * column + 3), 3)
 
         def video(step):
             @pl.when(tower == 0)
@@ -315,17 +423,35 @@
             for which in range(2):
                 pass_pair(which, chunk).start()
 
-            @pl.when(jnp.logical_not(is_last))
+            @pl.when(has_forward)
             def _():
                 for which in range(2):
                     pass_next(which, chunk).start()
 
-            @pl.when(step > 0)
+            @pl.when(past_edge)
+            def _():
+                for which in range(2):
+                    pass_back(which, chunk).start()
+
+            @pl.when(jnp.logical_and(step > 0, jnp.logical_not(late)))
             def _():
                 video(step - 1)
 
+            @pl.when(late)
+            def _():
+                for i in range(2):
+                    attend_edge(2 * step + i)
+
+            @pl.when(jnp.logical_and(tower == 0, is_last))
+            def _():
+                for i in range(2):
+                    relay(2 * step + i)
+
         loop(HALF, take)
-        video(HALF - 1)
+
+        @pl.when(jnp.logical_not(late))
+        def _():
+            video(HALF - 1)
 
         for which in range(2):
             own_copy(which).wait()
@@ -335,29 +461,31 @@
             dst = aud_q.at[:, cols(step)]
             remote(dst, dst, send_a.at[0, step], recv_q.at[step], tower, column).wait_recv()
 
-            @pl.when(jnp.logical_not(is_last))
+            @pl.when(has_forward)
             def _():
                 for which in range(2):
                     third_wait(which, step).wait_recv()
 
-            lane = lax.broadcasted_iota(jnp.int32, (BLOCK, DIM), 1)
-            stat = jnp.zeros((BLOCK, DIM), jnp.float32)
+            results = []
             for i in range(PER):
                 at = head_cols(step * PER + i)
                 mixed, top, total = mix(aud_q[:, at], aud_k[:, at], aud_v[:, at], audio_bias)
                 part_out[:, at] = mixed.astype(jnp.bfloat16)
-                stat = jnp.where(lane == 2 * i, top, stat)
-                stat = jnp.where(lane == 2 * i + 1, total, stat)
-            part_stat[step] = jnp.transpose(stat)[0:8]
+                results.append((top, total))
+            part_stat[step] = pack(results)
             stat_copy(step).start()
             part_copy(step).start()
 
+            @pl.when(late)
+            def _():
+                video(step)
+
         loop(HALF, audio)
 
         for which in range(2):
             pair_copy(which).wait_send()
 
-        @pl.when(jnp.logical_and(tower == 0, jnp.logical_not(is_first)))
+        @pl.when(jnp.logical_and(tower == 0, has_back))
         def _():
             def drain(chunk):
                 for half in range(2):
@@ -371,15 +499,37 @@
             for which in range(2):
                 pass_pair(which, chunk).wait_send()
 
-            @pl.when(jnp.logical_not(is_last))
+            @pl.when(has_forward)
             def _():
                 for which in range(2):
                     pass_next(which, chunk).wait_send()
+
+            @pl.when(past_edge)
+            def _():
+                for which in range(2):
+                    pass_back(which, chunk).wait_send()
 
             stat_copy(step).wait_send()
             part_copy(step).wait_send()
 
         loop(HALF, drain)
+
+        @pl.when(late)
+        def _():
+            def drain_edge(chunk):
+                edge_part(chunk).wait_send()
+                edge_stats(chunk).wait_send()
+
+            loop(CHUNKS, drain_edge)
+
+        @pl.when(jnp.logical_and(tower == 0, is_last))
+        def _():
+            def drain_relay(chunk):
+                for which in range(2):
+                    relay_copy(which, chunk).wait_send()
+
+            loop(CHUNKS, drain_relay)
+
         loop(CHUNKS, finish_out)
 
     @pl.when(tower == 2)
@@ -412,9 +562,27 @@
             for which in range(2):
                 next_copy(which, chunk).start()
 
-        @pl.when(jnp.logical_not(is_last))
+        def relay_in(which, chunk):
+            return remote(
+                sources[which].at[0, :, cols(chunk)],
+                (relay_k, relay_v)[which].at[:, cols(chunk)],
+                send_b.at[which, chunk],
+                recv_relay.at[which, chunk],
+                0,
+                last,
+            )
+
+        @pl.when(has_forward)
         def _():
             loop(CHUNKS, start_next)
+
+        @pl.when(at_edge)
+        def _():
+            def start_relay(chunk):
+                for which in range(2):
+                    relay_in(which, chunk).start()
+
+            loop(CHUNKS, start_relay)
 
         loop(CHUNKS, start_near)
 
@@ -423,8 +591,8 @@
             for ref in mains:
                 ref[BLOCK : 2 * BLOCK, :] = jnp.zeros((BLOCK, WIDTH), jnp.bfloat16)
 
-        q_copy.wait()
-        linked = jnp.logical_and(column < seq_count - 1, align_ref[after, 0] <= 3 * column + 2)
+        await_own()
+        linked = jnp.logical_and(column < seq_count - 1, align_ref[0, after] <= 3 * column + 2)
         bias = bias_row(linked, 2)
 
         def video(chunk):
@@ -442,10 +610,15 @@
             for which in range(2):
                 near_copy(which, chunk).wait_send()
 
-            @pl.when(jnp.logical_not(is_last))
+            @pl.when(has_forward)
             def _():
                 for which in range(2):
                     next_copy(which, chunk).wait_send()
+
+            @pl.when(at_edge)
+            def _():
+                for which in range(2):
+                    relay_in(which, chunk).wait_send()
 
             finish_out(chunk)
 
@@ -507,7 +680,41 @@
 
         loop(HALF, start_query)
 
-        @pl.when(jnp.logical_not(is_first))
+        def edge_query(chunk):
+            return remote(
+                q_hbm.at[0, :, cols(chunk)],
+                edge_q.at[:, cols(chunk)],
+                send_e.at[0, chunk],
+                recv_edge_q.at[chunk],
+                0,
+                edge + 1,
+            )
+
+        def edge_copy(which, chunk):
+            return remote(
+                sources[which].at[0, :, cols(chunk)],
+                mains[which].at[next_rows, cols(chunk)],
+                send_e.at[1 + which, chunk],
+                recv_next.at[which, chunk],
+                0,
+                edge + 1,
+            )
+
+        @pl.when(at_edge)
+        def _():
+            def start_queries(chunk):
+                edge_query(chunk).start()
+
+            loop(CHUNKS, start_queries)
+
+            def start_edge(step):
+                for half in range(2):
+                    for which in range(2):
+                        edge_copy(which, half * HALF + step).start()
+
+            loop(HALF, start_edge)
+
+        @pl.when(has_back)
         def _():
             def start_back(chunk):
                 for which in range(2):
@@ -526,8 +733,8 @@
             for ref in mains:
                 ref[BLOCK : 2 * BLOCK, :] = jnp.zeros((BLOCK, WIDTH), jnp.bfloat16)
 
-        q_copy.wait()
-        bias = bias_row(align_ref[column, 0] <= 3 * column - 1, 2)
+        await_own()
+        bias = bias_row(align_ref[0, column] <= 3 * column - 1, 2)
 
         def local(chunk):
             await_near(chunk)
@@ -546,13 +753,42 @@
 
         loop(CHUNKS, local)
 
+        def unpack(rows):
+            stat = jnp.concatenate([rows, jnp.zeros((DIM - 8, BLOCK), jnp.float32)], axis=0)
+            return jnp.transpose(stat)
+
+        @pl.when(at_edge)
+        def _():
+            reach = align_ref[1, column] > 3 * column + 3
+            shift = jnp.where(reach, 0.0, -jnp.inf).astype(jnp.float32)
+
+            def add_edge(chunk):
+                dst = edge_stat_in.at[chunk]
+                remote(dst, dst, send_a.at[0, chunk], recv_edge_stat.at[chunk], tower, column).wait_recv()
+                dst = edge_in.at[:, cols(chunk)]
+                remote(dst, dst, send_a.at[0, chunk], recv_edge.at[chunk], tower, column).wait_recv()
+                stat = unpack(edge_stat_in[chunk])
+                for i in range(PER):
+                    head = chunk * PER + i
+                    at = head_cols(head)
+                    far_top = stat[:, 2 * i : 2 * i + 1] + shift
+                    near_top = local_top[head][:, 0:1]
+                    top = jnp.maximum(far_top, near_top)
+                    far = jnp.exp2((far_top - top) * COLD)
+                    near = jnp.exp2((near_top - top) * COLD)
+                    total = far * stat[:, 2 * i + 1 : 2 * i + 2] + near * local_total[head][:, 0:1]
+                    local_mix[:, at] = edge_in[:, at].astype(jnp.float32) * far + local_mix[:, at] * near
+                    local_top[head] = jnp.broadcast_to(top, (BLOCK, DIM))
+                    local_total[head] = jnp.broadcast_to(total, (BLOCK, DIM))
+
+            loop(CHUNKS, add_edge)
+
         def merge_chunk(chunk):
             dst = stat_in.at[chunk]
             remote(dst, dst, send_a.at[0, chunk], recv_stat.at[chunk], tower, column).wait_recv()
             dst = part_in.at[:, cols(chunk)]
             remote(dst, dst, send_a.at[0, chunk], recv_part.at[chunk], tower, column).wait_recv()
-            stat = jnp.concatenate([stat_in[chunk], jnp.zeros((DIM - 8, BLOCK), jnp.float32)], axis=0)
-            stat = jnp.transpose(stat)
+            stat = unpack(stat_in[chunk])
             for i in range(PER):
                 head = chunk * PER + i
                 at = head_cols(head)
@@ -586,10 +822,16 @@
             for which in range(2):
                 near_copy(which, chunk).wait_send()
 
-            @pl.when(jnp.logical_not(is_first))
+            @pl.when(has_back)
             def _():
                 for which in range(2):
                     back_copy(which, chunk).wait_send()
+
+            @pl.when(at_edge)
+            def _():
+                edge_query(chunk).wait_send()
+                for which in range(2):
+                    edge_copy(which, chunk).wait_send()
 
             finish_out(chunk)
 
@@ -600,11 +842,12 @@
     bf16, f32 = jnp.bfloat16, jnp.float32
     dma = pltpu.SemaphoreType.DMA
     any_space = pl.BlockSpec(memory_space=pl.ANY)
-    smem = pl.BlockSpec(memory_space=pltpu.SMEM)
+    block = pltpu.VMEM((BLOCK, WIDTH), bf16)
+    hbm = pl.BlockSpec(memory_space=pltpu.HBM)
     return pl.pallas_call(
         functools.partial(kernel, seq_count),
         out_shape=jax.ShapeDtypeStruct(queries.shape, bf16),
-        in_specs=[smem, smem, any_space, any_space, any_space],
+        in_specs=[hbm] * 5,
         out_specs=any_space,
         scratch_shapes=[
             pltpu.VMEM((BLOCK, WIDTH), bf16),
@@ -621,7 +864,18 @@
             pltpu.VMEM((HEADS, BLOCK, DIM), f32),
             pltpu.VMEM((HEADS, BLOCK, DIM), f32),
             pltpu.VMEM((BLOCK, WIDTH), bf16),
-            dma((3,)),
+            pltpu.SMEM(alignment.shape[::-1], jnp.int32),
+            pltpu.SMEM(cross_gate.shape, f32),
+            block,
+            block,
+            block,
+            block,
+            pltpu.VMEM((CHUNKS, 8, BLOCK), f32),
+            block,
+            pltpu.VMEM((CHUNKS, 8, BLOCK), f32),
+            block,
+            block,
+            dma((7,)),
             dma((CHUNKS,)),
             dma((2, CHUNKS)),
             dma((2, CHUNKS)),
@@ -634,11 +888,16 @@
             dma((2, HALF)),
             dma((CHUNKS,)),
             dma((CHUNKS,)),
+            dma((3, CHUNKS)),
+            dma((CHUNKS,)),
+            dma((CHUNKS,)),
+            dma((CHUNKS,)),
+            dma((2, CHUNKS)),
         ],
         compiler_params=pltpu.CompilerParams(
-            collective_id=0, has_side_effects=True, vmem_limit_bytes=48 * 1024 * 1024
+            collective_id=0, has_side_effects=True, vmem_limit_bytes=52000000
         ),
-    )(alignment, cross_gate, queries, keys, values)
+    )(*(pltpu.with_memory_space_constraint(a, pltpu.HBM) for a in (jnp.transpose(alignment), cross_gate, queries, keys, values)))
 
 
 def solution(mesh):

time: 62.6 us -> 47.9 us (0.77)
  the two profiles are of different devices: /device:TPU:239 before, /device:TPU:251 now
where the time goes in v2:
time: 47.9 us; the launch traced here: 47.8 us
  Pallas kernels  46.9 us (98%)
  local copies, waits for them, and re-layouts  0.88 us (2%)
    pallas_call x1, Pallas kernels, local(): pl.pallas_call(functools.partial(kernel, seq_count), out_shape=jax.ShapeD...  46.9 us

profile of v2, /device:TPU:251, one launch (start us, length us, event | category | flops | bytes accessed | tf_op | source)
XLA Modules:
  0.0 47.8 jit_solution(10818795249599547974)
XLA Ops:
  0.0 46.9 %shard_map.55 = bf16[1,128,3072]{2,1,0:T(8,128)(2,1)S(1)} custom-call(s32[2,64]{1,0:T(2,128)} %bitcast.1, f32[2,24]{1,0:T(2,128)} %gate_hbm.1, bf16[1,128,3072]{2,1,0:T(8,128)(2,1)} %q_hbm.1, bf16[1,128,3072]{2,1,0:T(8,128)(2,1)} %k_hbm.1, bf16[1,128,3072]{2,1,0:T(8,128)(2,1)} %v_hbm.1), custom_call_target="tpu_custom_call" | custom-call | tf_op jit(solution)/shard_map/pallas_call | solution.py:847
  47.0 0.9 %copy.7 = bf16[1,128,3072]{2,1,0:T(8,128)(2,1)} copy(bf16[1,128,3072]{2,1,0:T(8,128)(2,1)S(1)} %shard_map.55) | data formatting | bytes 1572864

commit v3 on v2

--- a/solution.py
+++ b/solution.py
@@ -433,29 +433,23 @@
                 for which in range(2):
                     pass_back(which, chunk).start()
 
-            @pl.when(jnp.logical_and(step > 0, jnp.logical_not(late)))
-            def _():
-                video(step - 1)
+            @pl.when(jnp.logical_and(tower == 0, is_last))
+            def _():
+                for i in range(2):
+                    relay(2 * step + i)
+
+            @pl.when(step > 0)
+            def _():
+                @pl.when(jnp.logical_not(late))
+                def _():
+                    video(step - 1)
+
+                audio(step - 1)
 
             @pl.when(late)
             def _():
                 for i in range(2):
                     attend_edge(2 * step + i)
-
-            @pl.when(jnp.logical_and(tower == 0, is_last))
-            def _():
-                for i in range(2):
-                    relay(2 * step + i)
-
-        loop(HALF, take)
-
-        @pl.when(jnp.logical_not(late))
-        def _():
-            video(HALF - 1)
-
-        for which in range(2):
-            own_copy(which).wait()
-            pair_wait(which).wait_recv()
 
         def audio(step):
             dst = aud_q.at[:, cols(step)]
@@ -476,11 +470,18 @@
             stat_copy(step).start()
             part_copy(step).start()
 
-            @pl.when(late)
-            def _():
-                video(step)
-
-        loop(HALF, audio)
+        for which in range(2):
+            own_copy(which).wait()
+            pair_wait(which).wait_recv()
+
+        loop(HALF, take)
+        audio(HALF - 1)
+
+        def rest(step, carry):
+            video(step)
+            return carry
+
+        lax.fori_loop(jnp.where(late, 0, HALF - 1), HALF, rest, 0)
 
         for which in range(2):
             pair_copy(which).wait_send()
@@ -667,19 +668,6 @@
                 before,
             )
 
-        def start_far(step):
-            for half in range(2):
-                for which in range(2):
-                    far_copy(which, half, step).start()
-
-        loop(HALF, start_far)
-
-        def start_query(step):
-            for half in range(2):
-                query_copy(half, step).start()
-
-        loop(HALF, start_query)
-
         def edge_query(chunk):
             return remote(
                 q_hbm.at[0, :, cols(chunk)],
@@ -707,6 +695,22 @@
 
             loop(CHUNKS, start_queries)
 
+        def start_far(step):
+            for half in range(2):
+                for which in range(2):
+                    far_copy(which, half, step).start()
+
+            @pl.when(step > 0)
+            def _():
+                for half in range(2):
+                    query_copy(half, step - 1).start()
+
+        loop(HALF, start_far)
+        for half in range(2):
+            query_copy(half, HALF - 1).start()
+
+        @pl.when(at_edge)
+        def _():
             def start_edge(step):
                 for half in range(2):
                     for which in range(2):

time: 47.9 us -> 47.9 us (level)
  no operation moved by 1% of the time
where the time goes in v3:
time: 47.9 us; the launch traced here: 47.8 us
  Pallas kernels  46.9 us (98%)
  local copies, waits for them, and re-layouts  0.88 us (2%)
    pallas_call x1, Pallas kernels, local(): pl.pallas_call(functools.partial(kernel, seq_count), out_shape=jax.ShapeD...  46.9 us

profile of v3, /device:TPU:251, one launch (start us, length us, event | category | flops | bytes accessed | tf_op | source)
XLA Modules:
  0.0 47.8 jit_solution(13371157249402210906)
XLA Ops:
  0.0 46.9 %shard_map.55 = bf16[1,128,3072]{2,1,0:T(8,128)(2,1)S(1)} custom-call(s32[2,64]{1,0:T(2,128)} %bitcast.1, f32[2,24]{1,0:T(2,128)} %gate_hbm.1, bf16[1,128,3072]{2,1,0:T(8,128)(2,1)} %q_hbm.1, bf16[1,128,3072]{2,1,0:T(8,128)(2,1)} %k_hbm.1, bf16[1,128,3072]{2,1,0:T(8,128)(2,1)} %v_hbm.1), custom_call_target="tpu_custom_call" | custom-call | tf_op jit(solution)/shard_map/pallas_call | solution.py:851
  47.0 0.9 %copy.7 = bf16[1,128,3072]{2,1,0:T(8,128)(2,1)} copy(bf16[1,128,3072]{2,1,0:T(8,128)(2,1)S(1)} %shard_map.55) | data formatting | bytes 1572864

commit v4 on v3

--- a/solution.py
+++ b/solution.py
@@ -77,8 +77,6 @@
     out_buf,
     align_ref,
     gate_ref,
-    edge_k,
-    edge_v,
     edge_q,
     edge_out,
     edge_stat,
@@ -174,7 +172,7 @@
 
     @pl.when(tower == 1)
     def _():
-        meet((0, 3), [(has_forward, 0, after), (past_edge, 2, edge)])
+        meet((0, 3), [(has_forward, 0, after), (past_edge, 2, edge), (past_edge, 3, edge)])
 
     @pl.when(tower == 2)
     def _():
@@ -182,7 +180,7 @@
 
     @pl.when(tower == 3)
     def _():
-        meet((0, 1, 2), [(has_back, 2, before), (at_edge, 0, edge + 1), (past_edge, 0, last)])
+        meet((0, 1, 2), [(has_back, 2, before), (at_edge, 0, edge + 1), (at_edge, 1, edge + 1), (past_edge, 0, last)])
 
     near_rows = pl.ds(0, BLOCK)
     next_rows = pl.ds(BLOCK, BLOCK)
@@ -307,10 +305,7 @@
                 before,
             )
 
-        late = jnp.logical_and(tower == 0, past_edge)
-
-        def edge_own(which):
-            return pltpu.make_async_copy(sources[which].at[0], (edge_k, edge_v)[which], local_sem.at[5 + which])
+        lag = jnp.where(jnp.logical_and(tower == 0, past_edge), 2, 1)
 
         def edge_part(chunk):
             return remote(
@@ -330,13 +325,17 @@
                 stat = jnp.where(lane == 2 * i + 1, total, stat)
             return jnp.transpose(stat)[0:8]
 
-        def attend_edge(chunk):
+        def attend_edge(step):
+            chunk = own_base + step
             dst = edge_q.at[:, cols(chunk)]
             remote(dst, dst, send_e.at[0, chunk], recv_edge_q.at[chunk], tower, column).wait_recv()
             results = []
             for i in range(PER):
                 at = head_cols(chunk * PER + i)
-                mixed, top, total = mix(edge_q[:, at], edge_k[:, at], edge_v[:, at], None)
+                key_at = head_cols(step * PER + i)
+                mixed, top, total = mix(
+                    edge_q[:, at], aud_k[0:BLOCK, key_at], aud_v[0:BLOCK, key_at], None
+                )
                 edge_out[:, at] = mixed.astype(jnp.bfloat16)
                 results.append((top, total))
             edge_stat[chunk] = pack(results)
@@ -362,13 +361,6 @@
         for which in range(2):
             pair_copy(which).start()
 
-        @pl.when(late)
-        def _():
-            for which in range(2):
-                edge_own(which).start()
-            for which in range(2):
-                edge_own(which).wait()
-
         @pl.when(jnp.logical_and(tower == 0, has_back))
         def _():
             def start(chunk):
@@ -433,23 +425,22 @@
                 for which in range(2):
                     pass_back(which, chunk).start()
 
-            @pl.when(jnp.logical_and(tower == 0, is_last))
-            def _():
-                for i in range(2):
-                    relay(2 * step + i)
+            @pl.when(jnp.logical_and(jnp.logical_and(tower == 0, is_last), jnp.logical_and(step > 0, step < 5)))
+            def _():
+                for i in range(3):
+                    relay(3 * (step - 1) + i)
+
+            @pl.when(jnp.logical_and(past_edge, step > 0))
+            def _():
+                attend_edge(step - 1)
+
+            @pl.when(step >= lag)
+            def _():
+                video(step - lag)
 
             @pl.when(step > 0)
             def _():
-                @pl.when(jnp.logical_not(late))
-                def _():
-                    video(step - 1)
-
                 audio(step - 1)
-
-            @pl.when(late)
-            def _():
-                for i in range(2):
-                    attend_edge(2 * step + i)
 
         def audio(step):
             dst = aud_q.at[:, cols(step)]
@@ -475,13 +466,18 @@
             pair_wait(which).wait_recv()
 
         loop(HALF, take)
+
+        @pl.when(past_edge)
+        def _():
+            attend_edge(HALF - 1)
+
         audio(HALF - 1)
 
         def rest(step, carry):
             video(step)
             return carry
 
-        lax.fori_loop(jnp.where(late, 0, HALF - 1), HALF, rest, 0)
+        lax.fori_loop(HALF - lag, HALF, rest, 0)
 
         for which in range(2):
             pair_copy(which).wait_send()
@@ -515,13 +511,13 @@
 
         loop(HALF, drain)
 
-        @pl.when(late)
-        def _():
-            def drain_edge(chunk):
-                edge_part(chunk).wait_send()
-                edge_stats(chunk).wait_send()
-
-            loop(CHUNKS, drain_edge)
+        @pl.when(past_edge)
+        def _():
+            def drain_edge(step):
+                edge_part(own_base + step).wait_send()
+                edge_stats(own_base + step).wait_send()
+
+            loop(HALF, drain_edge)
 
         @pl.when(jnp.logical_and(tower == 0, is_last))
         def _():
@@ -668,13 +664,14 @@
                 before,
             )
 
-        def edge_query(chunk):
+        def edge_query(half, step):
+            chunk = half * HALF + step
             return remote(
                 q_hbm.at[0, :, cols(chunk)],
                 edge_q.at[:, cols(chunk)],
                 send_e.at[0, chunk],
                 recv_edge_q.at[chunk],
-                0,
+                half,
                 edge + 1,
             )
 
@@ -688,13 +685,6 @@
                 edge + 1,
             )
 
-        @pl.when(at_edge)
-        def _():
-            def start_queries(chunk):
-                edge_query(chunk).start()
-
-            loop(CHUNKS, start_queries)
-
         def start_far(step):
             for half in range(2):
                 for which in range(2):
@@ -704,19 +694,22 @@
             def _():
                 for half in range(2):
                     query_copy(half, step - 1).start()
+
+            @pl.when(jnp.logical_and(at_edge, step < HALF // 2))
+            def _():
+                for i in range(2):
+                    for half in range(2):
+                        edge_query(half, 2 * step + i).start()
+
+            @pl.when(at_edge)
+            def _():
+                for half in range(2):
+                    for which in range(2):
+                        edge_copy(which, half * HALF + step).start()
 
         loop(HALF, start_far)
         for half in range(2):
             query_copy(half, HALF - 1).start()
-
-        @pl.when(at_edge)
-        def _():
-            def start_edge(step):
-                for half in range(2):
-                    for which in range(2):
-                        edge_copy(which, half * HALF + step).start()
-
-            loop(HALF, start_edge)
 
         @pl.when(has_back)
         def _():
@@ -785,7 +778,11 @@
                     local_top[head] = jnp.broadcast_to(top, (BLOCK, DIM))
                     local_total[head] = jnp.broadcast_to(total, (BLOCK, DIM))
 
-            loop(CHUNKS, add_edge)
+            def add_both(step):
+                for half in range(2):
+                    add_edge(half * HALF + step)
+
+            loop(HALF, add_both)
 
         def merge_chunk(chunk):
             dst = stat_in.at[chunk]
@@ -820,6 +817,11 @@
                     far_copy(which, half, step).wait_send()
                 query_copy(half, step).wait_send()
 
+            @pl.when(at_edge)
+            def _():
+                for half in range(2):
+                    edge_query(half, step).wait_send()
+
         loop(HALF, drain_far)
 
         def drain(chunk):
@@ -833,7 +835,6 @@
 
             @pl.when(at_edge)
             def _():
-                edge_query(chunk).wait_send()
                 for which in range(2):
                     edge_copy(which, chunk).wait_send()
 
@@ -872,14 +873,12 @@
             pltpu.SMEM(cross_gate.shape, f32),
             block,
             block,
-            block,
-            block,
             pltpu.VMEM((CHUNKS, 8, BLOCK), f32),
             block,
             pltpu.VMEM((CHUNKS, 8, BLOCK), f32),
             block,
             block,
-            dma((7,)),
+            dma((5,)),
             dma((CHUNKS,)),
             dma((2, CHUNKS)),
             dma((2, CHUNKS)),

time: 47.9 us -> 47.9 us (level)
  no operation moved by 1% of the time
where the time goes in v4:
time: 47.9 us; the launch traced here: 47.8 us
  Pallas kernels  46.9 us (98%)
  local copies, waits for them, and re-layouts  0.88 us (2%)
    pallas_call x1, Pallas kernels, local(): pl.pallas_call(functools.partial(kernel, seq_count), out_shape=jax.ShapeD...  46.9 us

profile of v4, /device:TPU:251, one launch (start us, length us, event | category | flops | bytes accessed | tf_op | source)
XLA Modules:
  0.0 47.8 jit_solution(4375849246523776482)
XLA Ops:
  0.0 46.9 %shard_map.55 = bf16[1,128,3072]{2,1,0:T(8,128)(2,1)S(1)} custom-call(s32[2,64]{1,0:T(2,128)} %bitcast.1, f32[2,24]{1,0:T(2,128)} %gate_hbm.1, bf16[1,128,3072]{2,1,0:T(8,128)(2,1)} %q_hbm.1, bf16[1,128,3072]{2,1,0:T(8,128)(2,1)} %k_hbm.1, bf16[1,128,3072]{2,1,0:T(8,128)(2,1)} %v_hbm.1), custom_call_target="tpu_custom_call" | custom-call | tf_op jit(solution)/shard_map/pallas_call | solution.py:852
  47.0 0.9 %copy.7 = bf16[1,128,3072]{2,1,0:T(8,128)(2,1)} copy(bf16[1,128,3072]{2,1,0:T(8,128)(2,1)S(1)} %shard_map.55) | data formatting | bytes 1572864

commit v5 on v4

--- a/solution.py
+++ b/solution.py
@@ -109,6 +109,8 @@
     is_last = column == seq_count - 1
     edge = seq_count // 2 - 1
     last = seq_count - 1
+    hub = seq_count - 4
+    at_hub = column == hub
     at_edge = column == edge
     past_edge = column == edge + 1
     before = jnp.maximum(column - 1, 0)
@@ -163,8 +165,11 @@
                 (has_back, 0, before),
                 (has_back, 1, before),
                 (has_forward, 0, after),
-                (past_edge, 2, edge),
+                (past_edge, 0, hub),
                 (past_edge, 3, edge),
+                (at_hub, 0, edge + 1),
+                (at_hub, 1, edge + 1),
+                (at_hub, 2, edge),
                 (is_last, 2, edge),
                 (is_last, 3, edge + 1),
             ],
@@ -172,11 +177,11 @@
 
     @pl.when(tower == 1)
     def _():
-        meet((0, 3), [(has_forward, 0, after), (past_edge, 2, edge), (past_edge, 3, edge)])
+        meet((0, 3), [(has_forward, 0, after), (past_edge, 0, hub), (past_edge, 3, edge)])
 
     @pl.when(tower == 2)
     def _():
-        meet((3,), [(has_forward, 3, after), (at_edge, 0, edge + 1), (at_edge, 1, edge + 1), (at_edge, 0, last)])
+        meet((3,), [(has_forward, 3, after), (at_edge, 0, hub), (at_edge, 0, last)])
 
     @pl.when(tower == 3)
     def _():
@@ -298,11 +303,11 @@
         def pass_back(which, chunk):
             return remote(
                 mains[which].at[near_rows, cols(chunk)],
-                mains[which].at[next_rows, cols(chunk)],
+                (relay_k, relay_v)[which].at[:, cols(chunk)],
                 send_d.at[which, chunk],
-                recv_next.at[which, chunk],
-                2,
-                before,
+                recv_relay.at[which, chunk],
+                0,
+                hub,
             )
 
         lag = jnp.where(jnp.logical_and(tower == 0, past_edge), 2, 1)
@@ -348,8 +353,8 @@
                 mains[which].at[next_rows, cols(chunk)],
                 send_e.at[which, chunk],
                 recv_next.at[which, chunk],
-                3,
-                edge + 1,
+                jnp.where(is_last, 3, 2),
+                jnp.where(is_last, edge + 1, edge),
             )
 
         def relay(chunk):
@@ -429,6 +434,11 @@
             def _():
                 for i in range(3):
                     relay(3 * (step - 1) + i)
+
+            @pl.when(jnp.logical_and(jnp.logical_and(tower == 0, at_hub), step > 0))
+            def _():
+                for half in range(2):
+                    relay(half * HALF + step - 1)
 
             @pl.when(jnp.logical_and(past_edge, step > 0))
             def _():
@@ -467,6 +477,11 @@
 
         loop(HALF, take)
 
+        @pl.when(jnp.logical_and(tower == 0, at_hub))
+        def _():
+            for half in range(2):
+                relay(half * HALF + HALF - 1)
+
         @pl.when(past_edge)
         def _():
             attend_edge(HALF - 1)
@@ -519,7 +534,7 @@
 
             loop(HALF, drain_edge)
 
-        @pl.when(jnp.logical_and(tower == 0, is_last))
+        @pl.when(jnp.logical_and(tower == 0, jnp.logical_or(is_last, at_hub)))
         def _():
             def drain_relay(chunk):
                 for which in range(2):

time: 47.9 us -> 48 us (level)
  no operation moved by 1% of the time
where the time goes in v5:
time: 48 us; the launch traced here: 47.9 us
  Pallas kernels  47 us (98%)
  local copies, waits for them, and re-layouts  0.88 us (2%)
    pallas_call x1, Pallas kernels, local(): pl.pallas_call(functools.partial(kernel, seq_count), out_shape=jax.ShapeD...  47 us

profile of v5, /device:TPU:251, one launch (start us, length us, event | category | flops | bytes accessed | tf_op | source)
XLA Modules:
  0.0 47.9 jit_solution(17341063423376829613)
XLA Ops:
  0.0 47.0 %shard_map.55 = bf16[1,128,3072]{2,1,0:T(8,128)(2,1)S(1)} custom-call(s32[2,64]{1,0:T(2,128)} %bitcast.1, f32[2,24]{1,0:T(2,128)} %gate_hbm.1, bf16[1,128,3072]{2,1,0:T(8,128)(2,1)} %q_hbm.1, bf16[1,128,3072]{2,1,0:T(8,128)(2,1)} %k_hbm.1, bf16[1,128,3072]{2,1,0:T(8,128)(2,1)} %v_hbm.1), custom_call_target="tpu_custom_call" | custom-call | tf_op jit(solution)/shard_map/pallas_call | solution.py:867
  47.1 0.9 %copy.7 = bf16[1,128,3072]{2,1,0:T(8,128)(2,1)} copy(bf16[1,128,3072]{2,1,0:T(8,128)(2,1)S(1)} %shard_map.55) | data formatting | bytes 1572864
